TPU v7x, 256 devices: a whole 4x4x8 slice. The times are simulated.
256 devices in a mesh: grid: 16 (over y, x), mic: 4 (over z_hi), bin: 4 (over z_lo, core).
Axes of the slice: x: 4, y: 4, z: 8 (z_hi: 4, z_lo: 2; z = z_hi * 2 + z_lo), core: 2. Of those that a mesh axis runs over, the one named last changes fastest.
Arguments:
- grid_points: float32 [3, 16384], P(None, 'grid'), may hold values from -1 to 3, as said below
- mic_coords: float32 [3, 4096], P(None, 'mic'), may hold values from -1 to 1, as said below
- wavenumbers: float32 [16], P('bin'), may hold values from 20 to 150
- pressures: float32 [16, 2, 16, 4096], P('bin', None, None, 'mic'), may hold values from -6 to 6
Outputs:
- solution: float32 [16, 2, 16, 16384], P('bin', None, None, 'grid')
- residual: float32 [16, 2, 16, 4096], P('bin', None, None, 'mic')
Inputs may be any that keep to these rules, and one draw needn't show every extreme that they name: `grid_points`: rows 0 and 1 lie in -1 to 1, row 2 in 1 to 3. `mic_coords`: rows 0 and 1 lie in -1 to 1, row 2 in -0.05 to 0.05.
All inputs are finite; a program needn't handle non-finite values.
Results may differ from a plain program's by a relative error of at most 0.0055.
Values may be sent and summed in bfloat16 or wider, within the bound.
No kernel may reach another device: no remote copies, remote signals or barrier semaphores. Data moves between devices by JAX's collectives and lax.ppermute only.
A program may use at most 64 MiB of HBM per device.

v0:
```python
import math
import jax
import jax.numpy as jnp
from jax import lax
from jax.sharding import PartitionSpec as P

ITERS = 2


def steering_tiles(grid_points, mic_coords, wavenumbers, norm_scale):
    dist_x = grid_points[0][:, None] - mic_coords[0][None, :]
    dist_y = grid_points[1][:, None] - mic_coords[1][None, :]
    dist_z = grid_points[2][:, None] - mic_coords[2][None, :]
    radius = jnp.sqrt(dist_x * dist_x + dist_y * dist_y + dist_z * dist_z)
    amplitude = norm_scale / radius
    cos_list = []
    sin_list = []
    for bin_index in range(wavenumbers.shape[0]):
        phase_angle = wavenumbers[bin_index] * radius
        cos_list.append((jnp.cos(phase_angle) * amplitude).astype(jnp.bfloat16))
        sin_list.append((jnp.sin(phase_angle) * amplitude).astype(jnp.bfloat16))
    return (jnp.stack(cos_list), jnp.stack(sin_list))


def body(grid_points, mic_coords, wavenumbers, pressures):
    bin_count = pressures.shape[0]
    snap_count = pressures.shape[2]
    grid_local = grid_points.shape[1]
    norm_scale = 1.0 / math.sqrt(grid_local * lax.axis_size("grid"))
    cos_tiles, sin_tiles = steering_tiles(grid_points, mic_coords, wavenumbers, norm_scale)

    def combine_adjoint(cos_sum, sin_sum):
        real_part = cos_sum[:, :snap_count] - sin_sum[:, snap_count:]
        imag_part = cos_sum[:, snap_count:] + sin_sum[:, :snap_count]
        return jnp.stack([real_part, imag_part], axis=1)

    def apply_adjoint(residual):
        rounded = residual.astype(jnp.bfloat16).reshape(
            bin_count, 2 * snap_count, residual.shape[3]
        )
        cos_sum = jnp.einsum("fkm,fgm->fkg", rounded, cos_tiles, preferred_element_type=jnp.float32)
        sin_sum = jnp.einsum("fkm,fgm->fkg", rounded, sin_tiles, preferred_element_type=jnp.float32)
        partial_terms = combine_adjoint(cos_sum, sin_sum)
        summed = lax.psum(partial_terms, "mic")
        grad_norm = lax.psum(jnp.sum(summed * summed), ("grid", "bin"))
        return (summed, grad_norm)

    residual = pressures
    gradient, grad_norm = apply_adjoint(residual)
    direction = gradient
    solution = jnp.zeros_like(gradient)
    for iteration in range(ITERS):
        apply_rounded = direction.astype(jnp.bfloat16).reshape(
            bin_count, 2 * snap_count, direction.shape[3]
        )
        apply_cos_sum = jnp.einsum(
            "fkg,fgm->fkm", apply_rounded, cos_tiles, preferred_element_type=jnp.float32
        )
        apply_sin_sum = jnp.einsum(
            "fkg,fgm->fkm", apply_rounded, sin_tiles, preferred_element_type=jnp.float32
        )
        combine_real_part = apply_cos_sum[:, :snap_count] + apply_sin_sum[:, snap_count:]
        combine_imag_part = apply_cos_sum[:, snap_count:] - apply_sin_sum[:, :snap_count]
        apply_partial_terms = jnp.stack([combine_real_part, combine_imag_part], axis=1)
        apply_summed = lax.psum(apply_partial_terms, "grid")
        image_norm = lax.psum(jnp.sum(apply_summed * apply_summed), ("mic", "bin"))
        image, image_norm = (apply_summed, image_norm)
        step_size = grad_norm / image_norm
        solution = solution + step_size * direction
        residual = residual - step_size * image
        if iteration + 1 < ITERS:
            gradient, next_norm = apply_adjoint(residual)
            direction = gradient + next_norm / grad_norm * direction
            grad_norm = next_norm
    return (solution, residual)


def solution(mesh):
    placed = (P(None, "grid"), P(None, "mic"), P("bin"), P("bin", None, None, "mic"))
    return jax.shard_map(
        body,
        mesh=mesh,
        in_specs=placed,
        out_specs=(P("bin", None, None, "grid"), P("bin", None, None, "mic")),
        check_vma=False,
    )
```

profile of v0, /device:TPU:1, one launch (start us, length us, event | category | flops | bytes accessed | tf_op | source)
XLA Modules:
  0.0 768.9 jit_solution(6533060130410521625)
XLA Ops:
  7.2 1.5 fusion.13
  11.5 67.4 %multiply_convert_fusion.7 = (bf16[1,1024,1024]{2,1,0:T(8,128)(2,1)S(1)}, bf16[1,1024,1024]{2,1,0:T(8,128)(2,1)S(1)}, bf16[1,1024,1024]{2,1,0:T(8,128)(2,1)S(1)}...) fusion(f32[1024]{0:T(1024)S(1)} %bitcast.62, ...), kind=kLoop, calls=%fused_computation.9 | loop fusion | flops 30408704 | bytes 16801808 | tf_op jit(solution)/shard_map/convert_element_type | solution.py:20
  78.9 2.4 pad_maximum_fusion
  81.3 2.6 convolution_bitcast_fusion
  84.5 2.5 copy-done.2
  87.0 2.6 convolution_bitcast_fusion.1
  90.6 56.2 %all-reduce.5.cloned.1.call-done = f32[4,2,16,1024]{3,2,0,1:T(8,128)} async-done(((f32[4,2,16,1024]{3,2,0,1:T(8,128)}), f32[4,2,16,1024]{3,2,0,1:T(8,128)}) %all-reduce.5.cloned.1.call-update) | async-done | bytes 524304 | tf_op jit(solution)/shard_map/psum | solution.py:44
  146.7 1.9 multiply_reduce_fusion.3
  148.7 5.1 fusion.14
  154.5 1.5 fusion.15
  157.0 94.4 %all-reduce.7.cloned.1.call-done = f32[4,2,16,1024]{3,2,0,1:T(8,128)} async-done(((f32[4,2,16,1024]{3,2,0,1:T(8,128)}), f32[4,2,16,1024]{3,2,0,1:T(8,128)}) %all-reduce.7.cloned.1.call-update) | async-done | bytes 524304 | tf_op jit(solution)/shard_map/psum | solution.py:65
  251.4 1.8 multiply_reduce_fusion.2
  253.2 140.4 %psum.57 = f32[]{:T(128)} all-reduce(f32[]{:T(128)} %get-tuple-element.14), channel_id=1, replica_groups=mesh['grid'=16,'mic'=4,'bin'=4] {'grid','bin'}, use_global_device_ids=true, to_apply=%region_2.0 | all-reduce | flops 1 | bytes 8 | tf_op jit(solution)/shard_map/psum | solution.py:45
  393.6 25.9 %psum.59 = f32[]{:T(128)} all-reduce(f32[]{:T(128)} %multiply_reduce_fusion.2), channel_id=1, replica_groups=mesh['grid'=16,'mic'=4,'bin'=4] {'mic','bin'}, use_global_device_ids=true, to_apply=%region_5.0 | all-reduce | flops 1 | bytes 8 | tf_op jit(solution)/shard_map/psum | solution.py:66
  422.0 5.9 fusion.16
  427.9 6.0 fusion.17
  434.9 47.9 %all-reduce.9.cloned.1.call-done = f32[4,2,16,1024]{3,2,0,1:T(8,128)} async-done(((f32[4,2,16,1024]{3,2,0,1:T(8,128)}), f32[4,2,16,1024]{3,2,0,1:T(8,128)}) %all-reduce.9.cloned.1.call-update) | async-done | bytes 524304 | tf_op jit(solution)/shard_map/psum | solution.py:44
  482.8 1.8 multiply_reduce_fusion.1
  484.6 140.7 %psum.61 = f32[]{:T(128)} all-reduce(f32[]{:T(128)} %multiply_reduce_fusion.1), channel_id=1, replica_groups=mesh['grid'=16,'mic'=4,'bin'=4] {'grid','bin'}, use_global_device_ids=true, to_apply=%region_8.0 | all-reduce | flops 1 | bytes 8 | tf_op jit(solution)/shard_map/psum | solution.py:45
  627.8 4.9 fusion.18
  632.7 5.0 fusion.19
  638.6 91.7 %all-reduce.11.cloned.1.call-done = f32[4,2,16,1024]{3,2,0,1:T(8,128)} async-done(((f32[4,2,16,1024]{3,2,0,1:T(8,128)}), f32[4,2,16,1024]{3,2,0,1:T(8,128)}) %all-reduce.11.cloned.1.call-update) | async-done | bytes 524304 | tf_op jit(solution)/shard_map/psum | solution.py:65
  730.4 1.8 multiply_reduce_fusion
  732.1 26.0 %psum.63 = f32[]{:T(128)} all-reduce(f32[]{:T(128)} %multiply_reduce_fusion), channel_id=1, replica_groups=mesh['grid'=16,'mic'=4,'bin'=4] {'mic','bin'}, use_global_device_ids=true, to_apply=%region_11.0 | all-reduce | flops 1 | bytes 8 | tf_op jit(solution)/shard_map/psum | solution.py:66
  (41 shorter events, 13.2 us)
Async XLA Ops:
  7.2 139.6 %all-reduce.5.cloned.1.call-start = ((), (), s32[]{:S(2)}) async-start(), calls=%async_computation | async-start | bytes 1048576 | tf_op jit(solution)/shard_map/psum | solution.py:44
  81.3 3.2 copy-start
  81.3 5.7 copy-start.2
  90.5 160.9 %all-reduce.7.cloned.1.call-start = ((), (), s32[]{:S(2)}) async-start(), calls=%async_computation.1 | async-start | bytes 1048576 | tf_op jit(solution)/shard_map/psum | solution.py:65
  148.7 5.8 copy-start.1
  154.5 266.4 %copy-start.5 = (f32[4,2,16,1024]{3,2,1,0:T(8,128)S(1)}, f32[4,2,16,1024]{3,2,1,0:T(8,128)}, u32[]{:S(2)}) copy-start(f32[4,2,16,1024]{3,2,1,0:T(8,128)} %param.7) | copy-start | bytes 1572868
  156.9 325.9 %all-reduce.9.cloned.1.call-start = ((), (), s32[]{:S(2)}) async-start(), calls=%async_computation.2 | async-start | bytes 1048576 | tf_op jit(solution)/shard_map/psum | solution.py:44
  427.9 198.7 %copy-start.3 = (f32[4,2,16,1024]{3,2,0,1:T(8,128)S(1)}, f32[4,2,16,1024]{3,2,0,1:T(8,128)}, u32[]{:S(2)}) copy-start(f32[4,2,16,1024]{3,2,0,1:T(8,128)} %all-reduce.5.cloned.1.call-done) | copy-start | bytes 1572868
  434.9 295.5 %all-reduce.11.cloned.1.call-start = ((), (), s32[]{:S(2)}) async-start(), calls=%async_computation.3 | async-start | bytes 1048576 | tf_op jit(solution)/shard_map/psum | solution.py:65
  632.7 126.7 %copy-start.6 = (f32[4,2,16,1024]{3,2,0,1:T(8,128)S(1)}, f32[4,2,16,1024]{3,2,0,1:T(8,128)}, u32[]{:S(2)}) copy-start(f32[4,2,16,1024]{3,2,0,1:T(8,128)} %all-reduce.7.cloned.1.call-done) | copy-start | bytes 1572868
  637.7 123.8 %copy-start.4 = (f32[4,2,16,1024]{3,2,0,1:T(8,128)S(1)}, f32[4,2,16,1024]{3,2,0,1:T(8,128)}, u32[]{:S(2)}) copy-start(f32[4,2,16,1024]{3,2,0,1:T(8,128)} %all-reduce.9.cloned.1.call-done) | copy-start | bytes 1572868
Sparse Core Ops, SparseCore 0:
  90.6 56.0 all-reduce.4
  157.1 94.3 all-reduce.6
  435.0 47.7 all-reduce.8
  638.7 91.5 all-reduce.10
where the time goes:
time: 770 us; the launch traced here: 769 us
  blocking collectives  333 us (43%)
  waiting for transfers between devices  290 us (38%)
  other arithmetic  85.2 us (11%)
  matrix products  33.6 us (4%)
  between operations  17.9 us (2%)
  local copies, waits for them, and re-layouts  8.73 us (1%)
    psum x2, blocking collectives, apply_adjoint(): grad_norm = lax.psum(jnp.sum(summed * summed), ('grid', 'bin'))  281 us
    psum x2, waiting for transfers between devices, body(): apply_summed = lax.psum(apply_partial_terms, 'grid')  186 us
    psum x2, waiting for transfers between devices, apply_adjoint(): summed = lax.psum(partial_terms, 'mic')  104 us
    convert_element_type x1, other arithmetic, steering_tiles(): cos_list.append((jnp.cos(phase_angle) * amplitude).astype(jnp.bfloat16))  67.4 us
    psum x2, blocking collectives, body(): image_norm = lax.psum(jnp.sum(apply_summed * apply_summed), ('mic', 'bin'))  51.9 us
  transfers between devices with their start and end apart: 4, of which 4 were waited for; matrix products, arithmetic and copies ran while one was open for 0% of the time, Pallas kernels for 0%

commit v1 on v0

--- a/solution.py
+++ b/solution.py
@@ -62,7 +62,7 @@
         combine_real_part = apply_cos_sum[:, :snap_count] + apply_sin_sum[:, snap_count:]
         combine_imag_part = apply_cos_sum[:, snap_count:] - apply_sin_sum[:, :snap_count]
         apply_partial_terms = jnp.stack([combine_real_part, combine_imag_part], axis=1)
-        apply_summed = lax.psum(apply_partial_terms, "grid")
+        apply_summed = jnp.sum(lax.all_gather(apply_partial_terms, "grid"), axis=0)
         image_norm = lax.psum(jnp.sum(apply_summed * apply_summed), ("mic", "bin"))
         image, image_norm = (apply_summed, image_norm)
         step_size = grad_norm / image_norm

time: 770 us -> 738 us (0.958)
  waiting for transfers between devices: 290 us -> 254 us
    psum x2 -> x0, waiting for transfers between devices: 186 us -> none  [body(): apply_summed = lax.psum(apply_partial_terms, 'grid')]
    all_gather x0 -> x2, waiting for transfers between devices: none -> 150 us  [body(): apply_summed = jnp.sum(lax.all_gather(apply_partial_terms, 'grid'), axis=0)]
    reduce_sum x0 -> x2, other arithmetic: none -> 8.59 us  [body(): apply_summed = jnp.sum(lax.all_gather(apply_partial_terms, 'grid'), axis=0)]
where the time goes in v1:
time: 738 us; the launch traced here: 736 us
  blocking collectives  332 us (45%)
  waiting for transfers between devices  254 us (34%)
  other arithmetic  89.8 us (12%)
  matrix products  33.5 us (5%)
  between operations  17.8 us (2%)
  local copies, waits for them, and re-layouts  8.73 us (1%)
    psum x2, blocking collectives, apply_adjoint(): grad_norm = lax.psum(jnp.sum(summed * summed), ('grid', 'bin'))  280 us
    all_gather x2, waiting for transfers between devices, body(): apply_summed = jnp.sum(lax.all_gather(apply_partial_terms, 'grid'), axis=0)  150 us
    psum x2, waiting for transfers between devices, apply_adjoint(): summed = lax.psum(partial_terms, 'mic')  104 us
    convert_element_type x1, other arithmetic, steering_tiles(): cos_list.append((jnp.cos(phase_angle) * amplitude).astype(jnp.bfloat16))  67.5 us
    psum x2, blocking collectives, body(): image_norm = lax.psum(jnp.sum(apply_summed * apply_summed), ('mic', 'bin'))  52.2 us
  transfers between devices with their start and end apart: 4, of which 4 were waited for; matrix products, arithmetic and copies ran while one was open for 0% of the time, Pallas kernels for 0%

profile of v1, /device:TPU:1, one launch (start us, length us, event | category | flops | bytes accessed | tf_op | source)
XLA Modules:
  0.0 735.6 jit_solution(16639605374000150899)
XLA Ops:
  7.2 1.5 fusion.13
  11.5 67.5 %multiply_convert_fusion.7 = (bf16[1,1024,1024]{2,1,0:T(8,128)(2,1)S(1)}, bf16[1,1024,1024]{2,1,0:T(8,128)(2,1)S(1)}, bf16[1,1024,1024]{2,1,0:T(8,128)(2,1)S(1)}...) fusion(f32[1024]{0:T(1024)S(1)} %bitcast.66, ...), kind=kLoop, calls=%fused_computation.9 | loop fusion | flops 30408704 | bytes 16801808 | tf_op jit(solution)/shard_map/convert_element_type | solution.py:20
  78.9 2.4 pad_maximum_fusion
  81.3 2.6 convolution_bitcast_fusion
  84.5 2.5 copy-done.2
  87.0 2.6 convolution_bitcast_fusion.1
  90.6 55.9 %all-reduce.3.cloned.1.call-done = f32[4,2,16,1024]{3,2,0,1:T(8,128)} async-done(((f32[4,2,16,1024]{3,2,0,1:T(8,128)}), f32[4,2,16,1024]{3,2,0,1:T(8,128)}) %all-reduce.3.cloned.1.call-update) | async-done | bytes 524304 | tf_op jit(solution)/shard_map/psum | solution.py:44
  146.5 2.0 multiply_reduce_fusion.3
  148.5 5.1 fusion.14
  154.3 1.5 fusion.15
  156.8 76.3 %all-gather.5.cloned.1.call-done = f32[64,2,16,1024]{3,2,0,1:T(8,128)} async-done(((f32[4,2,16,1024]{3,2,0,1:T(8,128)}), f32[64,2,16,1024]{3,2,0,1:T(8,128)}) %all-gather.5.cloned.1.call-update) | async-done | bytes 8388624 | tf_op jit(solution)/shard_map/all_gather | solution.py:65
  233.1 4.3 reduce_sum.55
  238.1 139.1 %psum.43 = f32[]{:T(128)} all-reduce(f32[]{:T(128)} %get-tuple-element.14), channel_id=1, replica_groups=mesh['grid'=16,'mic'=4,'bin'=4] {'grid','bin'}, use_global_device_ids=true, to_apply=%region_2.0 | all-reduce | flops 1 | bytes 8 | tf_op jit(solution)/shard_map/psum | solution.py:45
  377.2 27.6 %psum.44 = f32[]{:T(128)} all-reduce(f32[]{:T(128)} %multiply_reduce_fusion.2), channel_id=1, replica_groups=mesh['grid'=16,'mic'=4,'bin'=4] {'mic','bin'}, use_global_device_ids=true, to_apply=%region_5.0 | all-reduce | flops 1 | bytes 8 | tf_op jit(solution)/shard_map/psum | solution.py:66
  406.2 5.9 fusion.16
  412.2 6.0 fusion.17
  419.2 47.9 %all-reduce.5.cloned.1.call-done = f32[4,2,16,1024]{3,2,0,1:T(8,128)} async-done(((f32[4,2,16,1024]{3,2,0,1:T(8,128)}), f32[4,2,16,1024]{3,2,0,1:T(8,128)}) %all-reduce.5.cloned.1.call-update) | async-done | bytes 524304 | tf_op jit(solution)/shard_map/psum | solution.py:44
  467.1 1.8 multiply_reduce_fusion.1
  468.9 140.6 %psum.46 = f32[]{:T(128)} all-reduce(f32[]{:T(128)} %multiply_reduce_fusion.1), channel_id=1, replica_groups=mesh['grid'=16,'mic'=4,'bin'=4] {'grid','bin'}, use_global_device_ids=true, to_apply=%region_8.0 | all-reduce | flops 1 | bytes 8 | tf_op jit(solution)/shard_map/psum | solution.py:45
  611.9 4.9 fusion.18
  616.8 4.9 fusion.19
  622.6 73.5 %all-gather.7.cloned.1.call-done = f32[64,2,16,1024]{3,2,0,1:T(8,128)} async-done(((f32[4,2,16,1024]{3,2,0,1:T(8,128)}), f32[64,2,16,1024]{3,2,0,1:T(8,128)}) %all-gather.7.cloned.1.call-update) | async-done | bytes 8388624 | tf_op jit(solution)/shard_map/all_gather | solution.py:65
  696.2 4.3 reduce_sum.58
  701.2 24.7 %psum.47 = f32[]{:T(128)} all-reduce(f32[]{:T(128)} %multiply_reduce_fusion), channel_id=1, replica_groups=mesh['grid'=16,'mic'=4,'bin'=4] {'mic','bin'}, use_global_device_ids=true, to_apply=%region_11.0 | all-reduce | flops 1 | bytes 8 | tf_op jit(solution)/shard_map/psum | solution.py:66
  (41 shorter events, 12.6 us)
Async XLA Ops:
  7.2 139.4 %all-reduce.3.cloned.1.call-start = ((), (), s32[]{:S(2)}) async-start(), calls=%async_computation | async-start | bytes 1048576 | tf_op jit(solution)/shard_map/psum | solution.py:44
  81.3 3.2 copy-start
  81.3 5.7 copy-start.2
  90.5 142.5 %all-gather.5.cloned.1.call-start = ((), (), s32[]{:S(2)}) async-start(), calls=%async_computation.2 | async-start | bytes 8912896 | tf_op jit(solution)/shard_map/all_gather | solution.py:65
  148.5 5.8 copy-start.1
  156.8 310.3 %all-reduce.5.cloned.1.call-start = ((), (), s32[]{:S(2)}) async-start(), calls=%async_computation.1 | async-start | bytes 1048576 | tf_op jit(solution)/shard_map/psum | solution.py:44
  233.1 173.0 %copy-start.5 = (f32[4,2,16,1024]{3,2,1,0:T(8,128)S(1)}, f32[4,2,16,1024]{3,2,1,0:T(8,128)}, u32[]{:S(2)}) copy-start(f32[4,2,16,1024]{3,2,1,0:T(8,128)} %param.7) | copy-start | bytes 1572868
  412.2 198.6 %copy-start.3 = (f32[4,2,16,1024]{3,2,0,1:T(8,128)S(1)}, f32[4,2,16,1024]{3,2,0,1:T(8,128)}, u32[]{:S(2)}) copy-start(f32[4,2,16,1024]{3,2,0,1:T(8,128)} %all-reduce.3.cloned.1.call-done) | copy-start | bytes 1572868
  419.1 277.1 %all-gather.7.cloned.1.call-start = ((), (), s32[]{:S(2)}) async-start(), calls=%async_computation.3 | async-start | bytes 8912896 | tf_op jit(solution)/shard_map/all_gather | solution.py:65
  696.2 31.9 %copy-start.4 = (f32[4,2,16,1024]{3,2,0,1:T(8,128)S(1)}, f32[4,2,16,1024]{3,2,0,1:T(8,128)}, u32[]{:S(2)}) copy-start(f32[4,2,16,1024]{3,2,0,1:T(8,128)} %all-reduce.5.cloned.1.call-done) | copy-start | bytes 1572868
Sparse Core Ops, SparseCore 0:
  90.7 55.8 all-reduce.2
  156.9 76.1 all-gather.4
  419.2 47.7 all-reduce.4
  622.8 73.3 all-gather.6
